TPU v7x, 32 devices: a whole 2x2x4 slice. The times are simulated.
32 devices in a mesh: frames: 4 (over y, core), win: 8 (over z, x).
Axes of the slice: x: 2, y: 2, z: 4, core: 2. Of those that a mesh axis runs over, the one named last changes fastest.
Arguments:
- memberships: float32 [8, 256, 4096], P('win', 'frames'), as said below
- lag_times: int32 [8], P('win'), may hold values from 1 to 8, as said below
- segment_ids: int32 [8, 256], P('win'), may hold values from 0 to 7, never falling along the last dimension, each value on 1 to 128 neighbouring positions
- bias_codes: int32 [8, 4096], P('win'), may hold values from 0 to 511
Outputs:
- free_energy: float32 [4096], P('frames')
- log_multipliers: float32 [8, 4096], P('win', 'frames')
Inputs may be any that keep to these rules, and one draw needn't show every extreme that they name: Positive; each frame's memberships sum to one up to rounding. `lag_times`: some window's lag time is 8.
All inputs are finite; a program needn't handle non-finite values.
Results may differ from a plain program's by a relative error of at most 0.00041.
Values may be sent and summed in bfloat16 or wider, within the bound.
No kernel may reach another device: no remote copies, remote signals or barrier semaphores. Data moves between devices by JAX's collectives and lax.ppermute only.
A program may use at most 64 MiB of HBM per device.

v0:
```python
import jax
import jax.numpy as jnp
from jax import lax
from jax.sharding import PartitionSpec as P

LAGMAX = 8
ITERS = 2
bias_unit = 1.0 / 128.0


def shifted(block, axis, distance):
    devices = range(lax.axis_size(axis))
    route = [(i - distance, i) for i in devices if i - distance in devices]
    return lax.ppermute(block, axis, route)


def split_rows(block, frames_dev, lag_time, valid_all):
    width = frames_dev + LAGMAX
    number = block.shape[0] // width
    states = block.shape[1]
    shaped = block.reshape(number, width, states)
    current = shaped[:, :frames_dev].reshape(number * frames_dev, states)
    later = lax.dynamic_slice_in_dim(shaped, lag_time, frames_dev, 1).reshape(
        number * frames_dev, states
    )
    later = jnp.where(valid_all[:, None], later, jnp.zeros((), later.dtype))
    return (current, later)


def add_pair(accumulated, current, later, first, rows):
    current_cols = lax.dynamic_slice_in_dim(current, first, rows, 1)
    later_cols = lax.dynamic_slice_in_dim(later, first, rows, 1)
    accumulated = jnp.einsum("tr,ts->rs", current_cols, later, preferred_element_type=jnp.float32)
    return accumulated + jnp.einsum(
        "tr,ts->rs", later_cols, current, preferred_element_type=jnp.float32
    )


def shards(memberships, lag_times, segment_ids, bias_codes):
    member = memberships[0].astype(jnp.bfloat16)
    lag_time = lag_times[0]
    segment_row = segment_ids[0]
    frames_dev = member.shape[0]
    states = member.shape[1]
    frames_all = segment_row.shape[0]
    rows = states // lax.axis_size("frames")
    position = lax.axis_index("frames")
    first = position * rows
    heading = shifted(member[:LAGMAX], "frames", -1)
    extended = jnp.concatenate([member, heading], axis=0)
    segment_ext = jnp.concatenate([segment_row, jnp.full((LAGMAX,), -1, jnp.int32)])
    valid_all = segment_row == lax.dynamic_slice_in_dim(segment_ext, lag_time, frames_all, 0)
    empty = jnp.zeros((rows, states), jnp.float32)
    current, later = split_rows(
        lax.all_gather(extended, "frames", axis=0, tiled=True), frames_dev, lag_time, valid_all
    )
    sym_counts = add_pair(empty, current, later, first, rows)
    gammas = jnp.exp(-bias_codes[0].astype(jnp.float32) * bias_unit)
    gamma_rows = lax.dynamic_slice_in_dim(gammas, first, rows, 0)
    mult_rows = jnp.sum(sym_counts, axis=1) * 0.5
    mult_full = lax.all_gather(mult_rows, "frames", axis=0, tiled=True)
    window_total = jnp.sum(mult_full)
    count_rows = lax.psum(mult_rows, "win")
    weights = jnp.full((states,), 1.0 / states, jnp.float32)
    for sweep in range(ITERS):
        scaled = gammas * weights
        scaled_rows = lax.dynamic_slice_in_dim(scaled, first, rows, 0)
        denom = mult_rows[:, None] * scaled[None, :] + scaled_rows[:, None] * mult_full[None, :]
        ratios = sym_counts / denom
        new_rows = mult_rows * jnp.sum(ratios * scaled[None, :], axis=1)
        terms = gamma_rows * jnp.sum(ratios * mult_full[None, :], axis=1)
        term_rows = lax.psum(terms, "win")
        raw_rows = count_rows / term_rows
        if sweep + 1 < ITERS:
            raw_full, mult_full = (
                lax.all_gather(raw_rows, "frames", axis=0, tiled=True),
                lax.all_gather(new_rows, "frames", axis=0, tiled=True),
            )
        else:
            raw_full = lax.all_gather(raw_rows, "frames", axis=0, tiled=True)
        weights = raw_full / jnp.sum(raw_full)
        mult_rows = new_rows
    weight_rows = lax.dynamic_slice_in_dim(weights, first, rows, 0)
    free_energy = -jnp.log(states * weight_rows)
    log_multipliers = jnp.log(mult_rows * states / window_total)[None, :]
    return (free_energy, log_multipliers)


def solution(mesh):
    placed = (P("win", "frames", None), P("win"), P("win", None), P("win", None))
    return jax.shard_map(
        shards,
        mesh=mesh,
        in_specs=placed,
        out_specs=(P("frames"), P("win", "frames")),
        check_vma=False,
    )
```

profile of v0, /device:TPU:0, one launch (start us, length us, event | category | flops | bytes accessed | tf_op | source)
XLA Modules:
  0.0 147.7 jit_solution(16507466639481832255)
XLA Ops:
  7.2 1.3 convert_element_type.11
  8.5 1.3 collective-permute-start
  9.8 1.3 convert_bitcast_fusion
  11.7 0.9 pad_maximum_fusion
  13.2 0.8 broadcast_multiply_fusion
  14.0 0.8 fusion.6
  14.8 25.7 %all-gather.2.cloned.1.call-done = bf16[288,4096]{1,0:T(8,128)(2,1)} async-done(((bf16[72,4096]{1,0:T(8,128)(2,1)}), bf16[288,4096]{1,0:T(8,128)(2,1)}) %all-gather.2.cloned.1.call-update) | async-done | bytes 2359312 | tf_op jit(solution)/shard_map/all_gather | solution.py:55
  40.5 2.9 %fusion.10 = (bf16[4,64,4096]{2,1,0:T(8,128)(2,1)S(1)}, bf16[4,64,4096]{2,1,0:T(8,128)(2,1)S(1)}) fusion(bf16[4,72,4096]{2,1,0:T(8,128)(2,1)} %bitcast.23, s32[]{:T(128)S(6)} %select_n.20), kind=kLoop, calls=%fused_computation.30 | loop fusion | bytes 8388612 | tf_op jit(solution)/shard_map/slice | solution.py:22
  43.8 0.9 copy-done.1
  44.8 8.1 %fusion.1 = f32[1024,4096]{1,0:T(8,128)} fusion(bf16[256,4096]{1,0:T(8,128)(2,1)S(1)} %bitcast_select_fusion, bf16[256,4096]{1,0:T(8,128)(2,1)S(1)} %bitcast.21, s32[]{:T(128)S(6)} %select_n.18), kind=kOutput, calls=%fused_computation.10 | convolution fusion | flops 2147483648 | bytes 19398660 | tf_op jit(solution)/shard_map/tr,ts->rs/dot_general | solution.py:33
  52.9 7.8 %fusion.11 = (f32[1024]{0:T(1024)S(1)}, f32[1024,4096]{1,0:T(8,128)S(1)}) fusion(f32[1024,4096]{1,0:T(8,128)} %fusion.1, bf16[256,4096]{1,0:T(8,128)(2,1)} %bitcast.22, bf16[256,4096]{1,0:T(8,128)(2,1)S(1)} %bitcast_select_fusion, s32[]{:T(128)S(6)} %select_n.18), kind=kOutput, calls=%fused_computation.31 | convolution fusion | flops 2155871232 | bytes 36179972 | tf_op jit(solution)/shard_map/tr,ts->rs/dot_general | solution.py:34
  60.7 5.2 %all_gather.16 = f32[4096]{0:T(1024)S(1)} all-gather(f32[1024]{0:T(1024)S(1)} %broadcast_multiply_fusion.1), channel_id=1, replica_groups=mesh['frames'=4,'win'=8] {'frames'}, dimensions={0}, use_global_device_ids=true | all-gather | bytes 20480 | tf_op jit(solution)/shard_map/all_gather | solution.py:61
  66.4 6.2 %multiply_reduce_fusion.2 = (f32[1024]{0:T(1024)S(1)}, f32[1024]{0:T(1024)S(1)}) fusion(f32[4096]{0:T(1024)S(1)} %all_gather.16, f32[4096]{0:T(1024)S(1)} %bitcast.26, f32[1024,4096]{1,0:T(8,128)S(1)} %get-tuple-element.13, f32[1024]{0:T(1024)S(1)} %dynamic-slice_multiply_fusion, f32[1024]{0:T(1024)S(1)} %broadcast_multiply_fusion.1), kind=kLoop, calls=%fused_computation.3 | loop fusion | flops 33552384 | bytes 16826368 | tf_op jit(solution)/shard_map/reduce_sum | solution.py:71
  72.6 5.2 %all_gather.18 = f32[4096]{0:T(1024)S(1)} all-gather(f32[1024]{0:T(1024)S(1)} %fusion.9), channel_id=1, replica_groups=mesh['frames'=4,'win'=8] {'frames'}, dimensions={0}, use_global_device_ids=true | all-gather | bytes 20480 | tf_op jit(solution)/shard_map/all_gather | solution.py:77
  77.8 21.6 %all-reduce.1 = (f32[1024]{0:T(1024)S(1)}, f32[1024]{0:T(1024)S(1)}) all-reduce(f32[1024]{0:T(1024)S(1)} %broadcast_multiply_fusion.1, f32[1024]{0:T(1024)S(1)} %mul.185), channel_id=1, replica_groups=mesh['frames'=4,'win'=8] {'win'}, use_global_device_ids=true, to_apply=%region_1.2 | all-reduce | flops 2048 | bytes 16384 | tf_op jit(solution)/shard_map/psum | solution.py:63
  99.4 5.2 %all_gather.17 = f32[4096]{0:T(1024)S(1)} all-gather(f32[1024]{0:T(1024)S(1)} %div.38), channel_id=1, replica_groups=mesh['frames'=4,'win'=8] {'frames'}, dimensions={0}, use_global_device_ids=true | all-gather | bytes 20480 | tf_op jit(solution)/shard_map/all_gather | solution.py:76
  105.2 0.6 reduce_sum.75
  105.8 0.7 divide_multiply_fusion
  106.5 9.0 %multiply_reduce_fusion = (f32[1024]{0:T(1024)S(1)}, f32[1024]{0:T(1024)S(1)}) fusion(f32[4096]{0:T(1024)S(1)} %divide_multiply_fusion, f32[4096]{0:T(1024)S(1)} %all_gather.18, f32[1024,4096]{1,0:T(8,128)} %copy-done, f32[1024]{0:T(1024)S(1)} %dynamic_slice.33, f32[1024]{0:T(1024)S(1)} %fusion.9), kind=kLoop, calls=%fused_computation | loop fusion | flops 33552384 | bytes 16826368 | tf_op jit(solution)/shard_map/reduce_sum | solution.py:70
  115.5 17.1 %psum.23 = f32[1024]{0:T(1024)S(1)} all-reduce(f32[1024]{0:T(1024)S(1)} %mul.193), channel_id=1, replica_groups=mesh['frames'=4,'win'=8] {'win'}, use_global_device_ids=true, to_apply=%region_7.8 | all-reduce | flops 1024 | bytes 8192 | tf_op jit(solution)/shard_map/psum | solution.py:72
  132.7 5.2 %all_gather.19 = f32[4096]{0:T(1024)S(1)} all-gather(f32[1024]{0:T(1024)S(1)} %div.42), channel_id=1, replica_groups=mesh['frames'=4,'win'=8] {'frames'}, dimensions={0}, use_global_device_ids=true | all-gather | bytes 20480 | tf_op jit(solution)/shard_map/all_gather | solution.py:80
  137.9 0.6 reduce_sum.77
  138.5 1.3 fusion.5
  139.7 1.2 divide_log_fusion
  (18 shorter events, 2.2 us)
Async XLA Ops:
  7.2 33.3 %all-gather.2.cloned.1.call-start = ((), (), s32[]{:S(2)}) async-start(), calls=%async_computation | async-start | bytes 2949120 | tf_op jit(solution)/shard_map/all_gather | solution.py:55
  8.5 3.1 %collective-permute-start = (bf16[8,4096]{1,0:T(8,128)(2,1)S(1)}, bf16[8,4096]{1,0:T(8,128)(2,1)S(1)}, u32[]{:S(2)}, u32[]{:S(2)}) collective-permute-start(bf16[8,4096]{1,0:T(8,128)(2,1)S(1)} %slice_bitcast_fusion), channel_id=1, source_target_pairs={{8,0},{16,8},{24,16},{9,1},{17,9},{25,17},{10,2},{18,10},{26,18},{... | collective-permute-start | bytes 196616 | tf_op jit(solution)/shard_map/ppermute | solution.py:14
  43.4 1.4 copy-start.1
  60.7 5.7 %copy-start = (f32[1024,4096]{1,0:T(8,128)}, f32[1024,4096]{1,0:T(8,128)S(1)}, u32[]{:S(2)}) copy-start(f32[1024,4096]{1,0:T(8,128)S(1)} %get-tuple-element.13) | copy-start | bytes 50331652
Sparse Core Ops, SparseCore 0:
  12.7 27.7 all-gather.1
where the time goes:
time: 148 us
  blocking collectives  59.6 us (40%)
  waiting for transfers between devices  26.2 us (18%)
  other arithmetic  25.5 us (17%)
  matrix products  15.9 us (11%)
  between operations  14.8 us (10%)
  local copies, waits for them, and re-layouts  4.38 us (3%)
    all_gather x1, waiting for transfers between devices, shards(): lax.all_gather(extended, 'frames', axis=0, tiled=True)  25.7 us
    psum x1, blocking collectives, shards(): count_rows = lax.psum(mult_rows, 'win')  21.6 us
    psum x1, blocking collectives, shards(): term_rows = lax.psum(terms, 'win')  17.1 us
    reduce_sum x1, other arithmetic, shards(): new_rows = mult_rows * jnp.sum(ratios * scaled[None, :], axis=1)  8.98 us
    dot_general x1, matrix products, add_pair(): jnp.einsum('tr,ts->rs', current_cols, later, preferred_element_type=jnp.f...  8.12 us
    dot_general x1, matrix products, add_pair(): jnp.einsum('tr,ts->rs', later_cols, current, preferred_element_type=jnp.f...  7.76 us
    reduce_sum x1, other arithmetic, shards(): terms = gamma_rows * jnp.sum(ratios * mult_full[None, :], axis=1)  6.19 us
    all_gather x1, blocking collectives, shards(): mult_full = lax.all_gather(mult_rows, 'frames', axis=0, tiled=True)  5.21 us
  transfers between devices with their start and end apart: 2, of which 2 were waited for; matrix products, arithmetic and copies ran while one was open for 2% of the time, Pallas kernels for 0%

commit v1 on v0

--- a/solution.py
+++ b/solution.py
@@ -51,9 +51,23 @@
     segment_ext = jnp.concatenate([segment_row, jnp.full((LAGMAX,), -1, jnp.int32)])
     valid_all = segment_row == lax.dynamic_slice_in_dim(segment_ext, lag_time, frames_all, 0)
     empty = jnp.zeros((rows, states), jnp.float32)
-    current, later = split_rows(
-        lax.all_gather(extended, "frames", axis=0, tiled=True), frames_dev, lag_time, valid_all
-    )
+
+    def derive_pieces_all(packet):
+        comm_axis = "frames"
+        n = jax.lax.axis_size(comm_axis)
+        slots = [(q, (q + 1) % n) for q in range(n)]
+        by_place = [(q, (q - 1) % n) for q in range(n)]
+        w1, current_arr = ([packet], [packet])
+        for _ in range(n // 2):
+            w1.append(jax.lax.ppermute(w1[-1], axis_name=comm_axis, perm=slots))
+        for _ in tuple(range((n - 1) // 2)):
+            current_arr.append(
+                jax.lax.ppermute(current_arr[-1], axis_name=comm_axis, perm=by_place)
+            )
+        long_array = jnp.concatenate([*w1[::-1], *current_arr[1:]], 0)
+        return jnp.roll(long_array, (jax.lax.axis_index(comm_axis) - n // 2) * packet.shape[0], 0)
+
+    current, later = split_rows(derive_pieces_all(extended), frames_dev, lag_time, valid_all)
     sym_counts = add_pair(empty, current, later, first, rows)
     gammas = jnp.exp(-bias_codes[0].astype(jnp.float32) * bias_unit)
     gamma_rows = lax.dynamic_slice_in_dim(gammas, first, rows, 0)

time: 148 us -> 131 us (0.89)
  between operations: 14.8 us -> 1.57 us
  waiting for transfers between devices: 26.2 us -> 18.7 us
  starting transfers between devices: 1.33 us -> 6.9 us
  local copies, waits for them, and re-layouts: 4.38 us -> 2.52 us
    all_gather x1 -> x0, waiting for transfers between devices: 25.7 us -> none  [shards(): lax.all_gather(extended, 'frames', axis=0, tiled=True)]
    ppermute x0 -> x3, waiting for transfers between devices: none -> 18.1 us  [the longest x2 13.6 us: derive_pieces_all(): w1.append(jax.lax.ppermute(w1[-1], axis_name=comm_axis, perm=slots))]
    ppermute x0 -> x3, starting transfers between devices: none -> 5.61 us  [the longest x2 3.87 us: derive_pieces_all(): w1.append(jax.lax.ppermute(w1[-1], axis_name=comm_axis, perm=slots))]
    slice x1, local copies, waits for them, and re-layouts: 2.92 us -> 0.7 us  [split_rows(): current = shaped[:, :frames_dev].reshape(number * frames_dev, states)]
  transfers between devices with their start and end apart: 2 -> 4, of which waited for: 2 -> 4; matrix products, arithmetic and copies ran while one was open for 2% -> 2% of each run, Pallas kernels for 0% -> 0%
where the time goes in v1:
time: 131 us
  blocking collectives  60.1 us (46%)
  other arithmetic  24.9 us (19%)
  waiting for transfers between devices  18.7 us (14%)
  matrix products  15.9 us (12%)
  starting transfers between devices  6.9 us (5%)
  local copies, waits for them, and re-layouts  2.52 us (2%)
  between operations  1.57 us (1%)
    psum x1, blocking collectives, shards(): count_rows = lax.psum(mult_rows, 'win')  21.9 us
    psum x1, blocking collectives, shards(): term_rows = lax.psum(terms, 'win')  17.1 us
    ppermute x2, waiting for transfers between devices, derive_pieces_all(): w1.append(jax.lax.ppermute(w1[-1], axis_name=comm_axis, perm=slots))  13.6 us
    reduce_sum x1, other arithmetic, shards(): new_rows = mult_rows * jnp.sum(ratios * scaled[None, :], axis=1)  8.98 us
    dot_general x1, matrix products, add_pair(): jnp.einsum('tr,ts->rs', current_cols, later, preferred_element_type=jnp.f...  8.12 us
    dot_general x1, matrix products, add_pair(): jnp.einsum('tr,ts->rs', later_cols, current, preferred_element_type=jnp.f...  7.77 us
    reduce_sum x1, other arithmetic, shards(): terms = gamma_rows * jnp.sum(ratios * mult_full[None, :], axis=1)  6.19 us
    all_gather x1, blocking collectives, shards(): mult_full = lax.all_gather(mult_rows, 'frames', axis=0, tiled=True)  5.46 us
  transfers between devices with their start and end apart: 4, of which 4 were waited for; matrix products, arithmetic and copies ran while one was open for 2% of the time, Pallas kernels for 0%

profile of v1, /device:TPU:0, one launch (start us, length us, event | category | flops | bytes accessed | tf_op | source)
XLA Modules:
  0.0 130.5 jit_solution(14376216983690428754)
XLA Ops:
  0.6 1.4 %convert_element_type.11 = bf16[1,64,4096]{2,1,0:T(8,128)(2,1)S(1)} convert(f32[1,64,4096]{2,1,0:T(8,128)} %param.4) | non-fusion elementwise | flops 262144 | bytes 1572864 | tf_op jit(solution)/shard_map/convert_element_type | solution.py:40
  2.0 1.3 collective-permute-start
  3.3 1.3 convert_bitcast_fusion
  5.2 3.9 %collective-permute-start.1 = (bf16[72,4096]{1,0:T(8,128)(2,1)S(1)}, bf16[72,4096]{1,0:T(8,128)(2,1)S(1)}, u32[]{:S(2)}, u32[]{:S(2)}) collective-permute-start(bf16[72,4096]{1,0:T(8,128)(2,1)S(1)} %pad_maximum_fusion), channel_id=1, source_target_pairs={{0,8},{8,16},{16,24},{24,0},{1,9},{9,17},{17,25},{25,1},{2,10},{10... | collective-permute-start | bytes 1769480 | tf_op jit(solution)/shard_map/ppermute | solution.py:62
  9.1 6.9 %collective-permute-done.1 = bf16[72,4096]{1,0:T(8,128)(2,1)S(1)} collective-permute-done((bf16[72,4096]{1,0:T(8,128)(2,1)S(1)}, bf16[72,4096]{1,0:T(8,128)(2,1)S(1)}, u32[]{:S(2)}, u32[]{:S(2)}) %collective-permute-start.1) | collective-permute-done | bytes 589856 | tf_op jit(solution)/shard_map/ppermute | solution.py:62
  16.0 0.7 broadcast_multiply_fusion
  17.5 0.8 fusion.8
  18.3 1.7 %collective-permute-start.3 = (bf16[72,4096]{1,0:T(8,128)(2,1)S(1)}, bf16[72,4096]{1,0:T(8,128)(2,1)S(1)}, u32[]{:S(2)}, u32[]{:S(2)}) collective-permute-start(bf16[72,4096]{1,0:T(8,128)(2,1)S(1)} %pad_maximum_fusion), channel_id=1, source_target_pairs={{0,24},{8,0},{16,8},{24,16},{1,25},{9,1},{17,9},{25,17},{2,26},{10... | collective-permute-start | bytes 1769480 | tf_op jit(solution)/shard_map/ppermute | solution.py:65
  20.1 6.7 %collective-permute-done.2 = bf16[72,4096]{1,0:T(8,128)(2,1)S(1)} collective-permute-done((bf16[72,4096]{1,0:T(8,128)(2,1)S(1)}, bf16[72,4096]{1,0:T(8,128)(2,1)S(1)}, u32[]{:S(2)}, u32[]{:S(2)}) %collective-permute-start.2) | collective-permute-done | bytes 589856 | tf_op jit(solution)/shard_map/ppermute | solution.py:62
  26.9 4.5 %collective-permute-done.3 = bf16[72,4096]{1,0:T(8,128)(2,1)S(1)} collective-permute-done((bf16[72,4096]{1,0:T(8,128)(2,1)S(1)}, bf16[72,4096]{1,0:T(8,128)(2,1)S(1)}, u32[]{:S(2)}, u32[]{:S(2)}) %collective-permute-start.3) | collective-permute-done | bytes 589856 | tf_op jit(solution)/shard_map/ppermute | solution.py:65
  32.3 0.7 fusion.10
  33.4 0.9 copy-done.2
  34.4 8.1 %fusion.1 = f32[1024,4096]{1,0:T(8,128)} fusion(bf16[256,4096]{1,0:T(8,128)(2,1)S(1)} %bitcast_select_fusion, bf16[256,4096]{1,0:T(8,128)(2,1)S(1)} %bitcast.24, s32[]{:T(128)S(6)} %select_n.33), kind=kOutput, calls=%fused_computation.10 | convolution fusion | flops 2147483648 | bytes 19398660 | tf_op jit(solution)/shard_map/tr,ts->rs/dot_general | solution.py:33
  42.5 7.8 %fusion.11 = (f32[1024]{0:T(1024)S(1)}, f32[1024,4096]{1,0:T(8,128)S(1)}) fusion(f32[1024,4096]{1,0:T(8,128)} %fusion.1, bf16[256,4096]{1,0:T(8,128)(2,1)} %bitcast.25, bf16[256,4096]{1,0:T(8,128)(2,1)S(1)} %bitcast_select_fusion, s32[]{:T(128)S(6)} %select_n.33), kind=kOutput, calls=%fused_computation.42 | convolution fusion | flops 2155871232 | bytes 36179972 | tf_op jit(solution)/shard_map/tr,ts->rs/dot_general | solution.py:34
  50.3 5.5 %all_gather.12 = f32[4096]{0:T(1024)S(1)} all-gather(f32[1024]{0:T(1024)S(1)} %broadcast_multiply_fusion.1), channel_id=1, replica_groups=mesh['frames'=4,'win'=8] {'frames'}, dimensions={0}, use_global_device_ids=true | all-gather | bytes 20480 | tf_op jit(solution)/shard_map/all_gather | solution.py:75
  55.7 6.2 %multiply_reduce_fusion.2 = (f32[1024]{0:T(1024)S(1)}, f32[1024]{0:T(1024)S(1)}) fusion(f32[4096]{0:T(1024)S(1)} %all_gather.12, f32[4096]{0:T(1024)S(1)} %bitcast.28, f32[1024,4096]{1,0:T(8,128)S(1)} %get-tuple-element.13, f32[1024]{0:T(1024)S(1)} %dynamic-slice_multiply_fusion, f32[1024]{0:T(1024)S(1)} %broadcast_multiply_fusion.1), kind=kLoop, calls=%fused_computation.3 | loop fusion | flops 33552384 | bytes 16826368 | tf_op jit(solution)/shard_map/reduce_sum | solution.py:85
  61.9 5.2 %all_gather.14 = f32[4096]{0:T(1024)S(1)} all-gather(f32[1024]{0:T(1024)S(1)} %fusion.9), channel_id=1, replica_groups=mesh['frames'=4,'win'=8] {'frames'}, dimensions={0}, use_global_device_ids=true | all-gather | bytes 20480 | tf_op jit(solution)/shard_map/all_gather | solution.py:91
  67.2 21.9 %all-reduce.1 = (f32[1024]{0:T(1024)S(1)}, f32[1024]{0:T(1024)S(1)}) all-reduce(f32[1024]{0:T(1024)S(1)} %broadcast_multiply_fusion.1, f32[1024]{0:T(1024)S(1)} %mul.189), channel_id=1, replica_groups=mesh['frames'=4,'win'=8] {'win'}, use_global_device_ids=true, to_apply=%region_1.2 | all-reduce | flops 2048 | bytes 16384 | tf_op jit(solution)/shard_map/psum | solution.py:77
  89.1 5.2 %all_gather.13 = f32[4096]{0:T(1024)S(1)} all-gather(f32[1024]{0:T(1024)S(1)} %div.38), channel_id=1, replica_groups=mesh['frames'=4,'win'=8] {'frames'}, dimensions={0}, use_global_device_ids=true | all-gather | bytes 20480 | tf_op jit(solution)/shard_map/all_gather | solution.py:90
  96.1 9.0 %multiply_reduce_fusion = (f32[1024]{0:T(1024)S(1)}, f32[1024]{0:T(1024)S(1)}) fusion(f32[4096]{0:T(1024)S(1)} %divide_multiply_fusion, f32[4096]{0:T(1024)S(1)} %all_gather.14, f32[1024,4096]{1,0:T(8,128)} %copy-done, f32[1024]{0:T(1024)S(1)} %dynamic_slice.38, f32[1024]{0:T(1024)S(1)} %fusion.9), kind=kLoop, calls=%fused_computation | loop fusion | flops 33552384 | bytes 16826368 | tf_op jit(solution)/shard_map/reduce_sum | solution.py:84
  105.1 17.1 %psum.23 = f32[1024]{0:T(1024)S(1)} all-reduce(f32[1024]{0:T(1024)S(1)} %mul.197), channel_id=1, replica_groups=mesh['frames'=4,'win'=8] {'win'}, use_global_device_ids=true, to_apply=%region_7.8 | all-reduce | flops 1024 | bytes 8192 | tf_op jit(solution)/shard_map/psum | solution.py:86
  122.3 5.2 %all_gather.15 = f32[4096]{0:T(1024)S(1)} all-gather(f32[1024]{0:T(1024)S(1)} %div.42), channel_id=1, replica_groups=mesh['frames'=4,'win'=8] {'frames'}, dimensions={0}, use_global_device_ids=true | all-gather | bytes 20480 | tf_op jit(solution)/shard_map/all_gather | solution.py:94
  128.1 1.3 fusion.5
  129.3 1.2 divide_log_fusion
  (34 shorter events, 4.5 us)
Async XLA Ops:
  0.6 26.2 %copy-start.1 = (f32[1,64,4096]{2,1,0:T(8,128)S(1)}, f32[1,64,4096]{2,1,0:T(8,128)}, u32[]{:S(2)}) copy-start(f32[1,64,4096]{2,1,0:T(8,128)} %param.4) | copy-start | bytes 3145732
  2.0 3.1 %collective-permute-start = (bf16[8,4096]{1,0:T(8,128)(2,1)S(1)}, bf16[8,4096]{1,0:T(8,128)(2,1)S(1)}, u32[]{:S(2)}, u32[]{:S(2)}) collective-permute-start(bf16[8,4096]{1,0:T(8,128)(2,1)S(1)} %slice_bitcast_fusion), channel_id=1, source_target_pairs={{8,0},{16,8},{24,16},{9,1},{17,9},{25,17},{10,2},{18,10},{26,18},{... | collective-permute-start | bytes 196616 | tf_op jit(solution)/shard_map/ppermute | solution.py:14
  5.2 10.8 %collective-permute-start.1 = (bf16[72,4096]{1,0:T(8,128)(2,1)S(1)}, bf16[72,4096]{1,0:T(8,128)(2,1)S(1)}, u32[]{:S(2)}, u32[]{:S(2)}) collective-permute-start(bf16[72,4096]{1,0:T(8,128)(2,1)S(1)} %pad_maximum_fusion), channel_id=1, source_target_pairs={{0,8},{8,16},{16,24},{24,0},{1,9},{9,17},{17,25},{25,1},{2,10},{10... | collective-permute-start | bytes 1769480 | tf_op jit(solution)/shard_map/ppermute | solution.py:62
  16.0 10.8 %collective-permute-start.2 = (bf16[72,4096]{1,0:T(8,128)(2,1)S(1)}, bf16[72,4096]{1,0:T(8,128)(2,1)S(1)}, u32[]{:S(2)}, u32[]{:S(2)}) collective-permute-start(bf16[72,4096]{1,0:T(8,128)(2,1)S(1)} %collective-permute-done.1), channel_id=1, source_target_pairs={{0,8},{8,16},{16,24},{24,0},{1,9},{9,17},{17,25},{25,1},{2,10},{10... | collective-permute-start | bytes 1769480 | tf_op jit(solution)/shard_map/ppermute | solution.py:62
  18.3 13.1 %collective-permute-start.3 = (bf16[72,4096]{1,0:T(8,128)(2,1)S(1)}, bf16[72,4096]{1,0:T(8,128)(2,1)S(1)}, u32[]{:S(2)}, u32[]{:S(2)}) collective-permute-start(bf16[72,4096]{1,0:T(8,128)(2,1)S(1)} %pad_maximum_fusion), channel_id=1, source_target_pairs={{0,24},{8,0},{16,8},{24,16},{1,25},{9,1},{17,9},{25,17},{2,26},{10... | collective-permute-start | bytes 1769480 | tf_op jit(solution)/shard_map/ppermute | solution.py:65
  33.0 1.4 %copy-start.2 = (bf16[4,64,4096]{2,1,0:T(8,128)(2,1)}, bf16[4,64,4096]{2,1,0:T(8,128)(2,1)S(1)}, u32[]{:S(2)}) copy-start(bf16[4,64,4096]{2,1,0:T(8,128)(2,1)S(1)} %get-tuple-element.10) | copy-start | bytes 6291460
  50.2 11.7 %copy-start = (f32[1024,4096]{1,0:T(8,128)}, f32[1024,4096]{1,0:T(8,128)S(1)}, u32[]{:S(2)}) copy-start(f32[1024,4096]{1,0:T(8,128)S(1)} %get-tuple-element.13) | copy-start | bytes 50331652
